TPU v7x, 32 devices: a whole 2x2x4 slice. The times are simulated.
32 devices in a mesh: groups: 2 (over x), tm: 8 (over z, y), rows: 2 (over core).
Axes of the slice: x: 2, y: 2, z: 4, core: 2. Of those that a mesh axis runs over, the one named last changes fastest.
Arguments:
- iterate: float32 [32, 512, 512], P(('groups', 'tm'), 'rows'), parts along dimension 0, may hold values from -6 to 6
- forcing: float32 [32, 512, 512], P(('groups', 'tm'), 'rows'), parts along dimension 0, may hold values from -18 to 18
- initial_state: float32 [1024, 512], P(('groups', 'rows')), parts along dimension 0, may hold values from -6 to 6
- diffusivity: float32 [1024, 512], P(('groups', 'rows')), parts along dimension 0, may hold values from 0.5 to 4
Outputs:
- updated: float32 [32, 512, 512], P(('groups', 'tm'), 'rows'), parts along dimension 0
- residual_rms: float32 [32], P(('groups', 'tm')), parts along dimension 0
There are 2 independent parts, one for each index of `groups`. A program takes and returns all parts, laid end to end along the dimension named above; each array names one. Nothing has to cross between parts.
All inputs are finite; a program needn't handle non-finite values.
Results may differ from a plain program's by a relative error of at most 0.0003.
Values sent between devices are 32-bit elements; how exact they have to be, the bound alone decides.
No kernel may reach another device: no remote copies, remote signals or barrier semaphores. Data moves between devices by JAX's collectives and lax.ppermute only.
A program may use at most 64 MiB of HBM per device.

v0:
```python
import jax
import jax.numpy as jnp
from jax import lax
from jax.sharding import PartitionSpec as P

CG_ITERS = 3
circulant_alpha = 0.05
time_step = 0.5
rms_eps = 1e-06


def extended(block, sides, width):
    for axis, dim in sides:
        count = lax.axis_size(axis)
        forward = [(i, i + 1) for i in range(count - 1)]
        backward = [(target, source) for source, target in forward]
        low = lax.ppermute(
            lax.slice_in_dim(block, block.shape[dim] - width, None, axis=dim), axis, forward
        )
        high = lax.ppermute(lax.slice_in_dim(block, 0, width, axis=dim), axis, backward)
        block = jnp.concatenate([low, block, high], axis=dim)
    return block


def from_behind(value, axis, steps):
    count = lax.axis_size(axis)
    initial, last = (max(0, -steps), min(count, count - steps))
    return lax.ppermute(value, axis, [(source, source + steps) for source in range(initial, last)])


def phase_table(first_index, second_index, length):
    product = first_index[:, None] * second_index[None, :] % length
    return 2.0 * jnp.pi / length * product.astype(jnp.float32)


def faces_from(padded_rows):
    centre = padded_rows[1:-1]
    columns = jnp.pad(centre, ((0, 0), (1, 1)), mode="edge")
    north_face = 0.5 * (centre + padded_rows[:-2])
    south_face = 0.5 * (centre + padded_rows[2:])
    west_face = 0.5 * (centre + columns[:, :-2])
    east_face = 0.5 * (centre + columns[:, 2:])
    return (north_face, south_face, west_face, east_face)


def apply_faces(padded_rows, weights):
    north_face, south_face, west_face, east_face = weights
    centre = padded_rows[..., 1:-1, :]
    lead_pad = [(0, 0)] * (centre.ndim - 1)
    columns = jnp.pad(centre, lead_pad + [(1, 1)])
    return (
        (north_face + south_face + west_face + east_face) * centre
        - north_face * padded_rows[..., :-2, :]
        - south_face * padded_rows[..., 2:, :]
        - west_face * columns[..., :-2]
        - east_face * columns[..., 2:]
    )


def high_dot(first_mat, second_mat):
    return jnp.dot(
        first_mat, second_mat, precision=lax.Precision.HIGHEST, preferred_element_type=jnp.float32
    )


def shards(iterate, forcing, initial_state, diffusivity):
    steps_dev, rows_dev, columns_dev = iterate.shape
    time_devices = lax.axis_size("tm")
    row_devices = lax.axis_size("rows")
    time_rank = lax.axis_index("tm")
    row_rank = lax.axis_index("rows")
    length = steps_dev * time_devices
    cell_count = rows_dev * row_devices * columns_dev
    rimmed = extended(diffusivity, (("rows", 0),), 1)
    top_row = jnp.where(row_rank == 0, diffusivity[:1], rimmed[:1])
    bottom_row = jnp.where(row_rank == row_devices - 1, diffusivity[-1:], rimmed[-1:])
    rimmed = jnp.concatenate([top_row, rimmed[1:-1], bottom_row], axis=0)
    local_faces = faces_from(rimmed)
    arriving = from_behind(iterate[-1], "tm", 1)
    first_previous = jnp.where(time_rank == 0, initial_state, arriving)
    previous = jnp.concatenate([first_previous[None], iterate[:-1]], axis=0)
    iterate_rim = extended(iterate, (("rows", 1),), 1)
    residual = (
        time_step * forcing + previous - iterate - time_step * apply_faces(iterate_rim, local_faces)
    )
    squares = lax.psum(jnp.sum(residual * residual, axis=(1, 2)), "rows")
    residual_rms = jnp.sqrt(squares / cell_count + rms_eps)
    step_index = time_rank * steps_dev + jnp.arange(steps_dev, dtype=jnp.int32)
    log_alpha = jnp.log(jnp.float32(circulant_alpha))
    growth = jnp.exp(log_alpha * step_index.astype(jnp.float32) / length)
    scaled = residual * growth[:, None, None]
    by_cells = lax.all_to_all(scaled, "tm", split_axis=1, concat_axis=0, tiled=True)
    slab_rows = by_cells.shape[1]
    all_index = jnp.arange(length, dtype=jnp.int32)
    angles = phase_table(all_index, all_index, length)
    flat_cells = by_cells.reshape(length, slab_rows * columns_dev)
    spectrum_real = high_dot(jnp.cos(angles), flat_cells)
    spectrum_imag = high_dot(-jnp.sin(angles), flat_cells)
    spectrum = jnp.stack([spectrum_real, spectrum_imag]).reshape(2, length, slab_rows, columns_dev)
    by_freq = lax.all_to_all(spectrum, "tm", split_axis=1, concat_axis=2, tiled=True)
    freq_index = time_rank * steps_dev + jnp.arange(steps_dev, dtype=jnp.int32)

    def rim_rows(values):
        return extended(values, (("rows", 2),), 1)

    def reduce_sums(values):
        return lax.psum(values, "rows")

    root_alpha = jnp.exp(log_alpha / length)
    freq_angle = 2.0 * jnp.pi / length * freq_index.astype(jnp.float32)
    real_shift = (1.0 - root_alpha * jnp.cos(freq_angle))[:, None, None]
    imag_shift = (root_alpha * jnp.sin(freq_angle))[:, None, None]

    def operate(values, orientation):
        spread = time_step * apply_faces(rim_rows(values), local_faces)
        swapped = jnp.stack([-values[1], values[0]])
        return real_shift * values + orientation * imag_shift * swapped + spread

    def freq_norm(values):
        return jnp.sum(values * values, axis=(0, 2, 3))

    def expand(values):
        return values[None, :, None, None]

    solution = jnp.zeros_like(by_freq)
    normal = operate(by_freq, -1.0)
    gamma_now = reduce_sums(freq_norm(normal))
    search = normal
    remain = by_freq
    for iteration in range(CG_ITERS):
        image_now = operate(search, 1.0)
        step_rate = gamma_now / reduce_sums(freq_norm(image_now))
        solution = solution + expand(step_rate) * search
        if iteration + 1 < CG_ITERS:
            remain = remain - expand(step_rate) * image_now
            normal = operate(remain, -1.0)
            gamma_next = reduce_sums(freq_norm(normal))
            search = normal + expand(gamma_next / gamma_now) * search
            gamma_now = gamma_next
    back_cells = lax.all_to_all(solution, "tm", split_axis=2, concat_axis=1, tiled=True)
    inverse_angles = phase_table(all_index, all_index, length)
    flat_real = back_cells[0].reshape(length, slab_rows * columns_dev)
    flat_imag = back_cells[1].reshape(length, slab_rows * columns_dev)
    correction = high_dot(jnp.cos(inverse_angles) / length, flat_real) - high_dot(
        jnp.sin(inverse_angles) / length, flat_imag
    )
    correction = correction.reshape(length, slab_rows, columns_dev)
    own_steps = lax.all_to_all(correction, "tm", split_axis=0, concat_axis=1, tiled=True)
    updated = iterate + own_steps / growth[:, None, None]
    return (updated, residual_rms)


def solution(mesh):
    placed = (
        P(("groups", "tm"), "rows", None),
        P(("groups", "tm"), "rows", None),
        P(("groups", "rows"), None),
        P(("groups", "rows"), None),
    )
    return jax.shard_map(
        shards,
        mesh=mesh,
        in_specs=placed,
        out_specs=(P(("groups", "tm"), "rows", None), P(("groups", "tm"))),
        check_vma=False,
    )
```

profile of v0, /device:TPU:0, one launch (start us, length us, event | category | flops | bytes accessed | tf_op | source)
XLA Modules:
  0.0 287.9 jit_solution(17938583159256987728)
XLA Ops:
  3.5 3.0 %collective-permute-start.3 = (f32[2,1,512]{2,1,0:T(1,128)S(1)}, f32[2,1,512]{2,1,0:T(1,128)S(1)}, u32[]{:S(2)}, u32[]{:S(2)}) collective-permute-start(f32[2,1,512]{2,1,0:T(1,128)S(1)} %get-tuple-element.53), channel_id=1, source_target_pairs={{0,1},{2,3},{4,5},{6,7},{8,9},{10,11},{12,13},{14,15},{16,17},{18,... | collective-permute-start | bytes 12296 | tf_op jit(solution)/shard_map/ppermute | solution.py:17
  9.9 5.1 %collective-permute-start = (f32[256,512]{1,0:T(8,128)}, f32[256,512]{1,0:T(8,128)S(1)}, u32[]{:S(2)}, u32[]{:S(2)}) collective-permute-start(f32[256,512]{1,0:T(8,128)} %get-tuple-element.51), channel_id=1, source_target_pairs={{0,2},{2,4},{4,6},{6,8},{8,10},{10,12},{12,14},{1,3},{3,5},{5,7},{... | collective-permute-start | bytes 1572872 | tf_op jit(solution)/shard_map/ppermute | solution.py:28
  15.1 2.7 collective-permute-start.1
  19.1 8.3 %collective-permute-done = f32[256,512]{1,0:T(8,128)S(1)} collective-permute-done((f32[256,512]{1,0:T(8,128)}, f32[256,512]{1,0:T(8,128)S(1)}, u32[]{:S(2)}, u32[]{:S(2)}) %collective-permute-start) | collective-permute-done | bytes 524320 | tf_op jit(solution)/shard_map/ppermute | solution.py:28
  29.6 32.5 %all_to_all.66 = f32[2,256,512]{2,0,1:T(2,128)S(1)} all-to-all(f32[2,256,512]{2,0,1:T(2,128)S(1)} %copy.31), channel_id=1, replica_groups=mesh['groups'=2,'tm'=8,'rows'=2] {'tm'}, dimensions={1} | all-to-all | bytes 2097152 | tf_op jit(solution)/shard_map/all_to_all | solution.py:92
  65.7 2.6 copy.35
  68.2 3.6 %all-to-all-start.1 = ((f32[2,16,32,512]{3,2,0,1:T(8,128)}), f32[2,16,32,512]{3,2,0,1:T(8,128)S(1)}, u32[]{:S(2)}, u32[]{:S(2)}) async-start(f32[2,16,32,512]{3,2,0,1:T(8,128)} %copy.35), calls=%async_computation.1 | async-start | bytes 4194304 | tf_op jit(solution)/shard_map/all_to_all | solution.py:100
  72.0 47.8 %all-to-all-done.1 = f32[2,16,32,512]{3,2,0,1:T(8,128)S(1)} async-done(((f32[2,16,32,512]{3,2,0,1:T(8,128)}), f32[2,16,32,512]{3,2,0,1:T(8,128)S(1)}, u32[]{:S(2)}, u32[]{:S(2)}) %all-to-all-start.1) | async-done | bytes 2097184 | tf_op jit(solution)/shard_map/all_to_all | solution.py:100
  124.6 2.5 multiply_reduce_fusion.4
  127.1 3.0 %collective-permute-start.7 = (f32[2,2,1,512]{3,2,1,0:T(1,128)S(1)}, f32[2,2,1,512]{3,2,1,0:T(1,128)S(1)}, u32[]{:S(2)}, u32[]{:S(2)}) collective-permute-start(f32[2,2,1,512]{3,2,1,0:T(1,128)S(1)} %get-tuple-element.45), channel_id=1, source_target_pairs={{0,1},{2,3},{4,5},{6,7},{8,9},{10,11},{12,13},{14,15},{16,17},{18,... | collective-permute-start | bytes 24584 | tf_op jit(solution)/shard_map/ppermute | solution.py:17
  133.2 3.4 %multiply_reduce_fusion.3 = (f32[2]{0:T(128)S(1)}, f32[2,2,256,512]{3,2,1,0:T(8,128)}) fusion(f32[256,512]{1,0:T(8,128)S(1)} %copy-done.15, f32[2,2,256,512]{3,2,1,0:T(8,128)S(1)} %get-tuple-element.19, f32[256,512]{1,0:T(8,128)S(1)} %copy-done.9, f32[2,2,1,512]{3,2,1,0:T(1,128)S(1)} %collective-permute-done.8, f32[256,512]{1,0:T(8,128)S(1)} %copy-done.3, ...), kind=kLoop, calls=%fused_computation.109 | loop fusion | flops 9961470 | bytes 8929304 | tf_op jit(solution)/shard_map/reduce_sum | solution.py:120
  136.6 2.4 all-reduce.8
  139.1 2.8 multiply_subtract_fusion.1
  141.9 2.1 collective-permute-start.9
  147.2 3.5 %multiply_reduce_fusion.2 = (f32[2]{0:T(128)S(1)}, f32[2,2,256,512]{3,2,1,0:T(8,128)}) fusion(f32[256,512]{1,0:T(8,128)S(1)} %copy-done.16, f32[2,2,256,512]{3,2,1,0:T(8,128)S(1)} %multiply_subtract_fusion.1, f32[256,512]{1,0:T(8,128)S(1)} %copy-done.10, f32[2,2,1,512]{3,2,1,0:T(1,128)S(1)} %collective-permute-done.10, f32[256,512]{1,0:T(8,128)S(1)} %copy-done.4, ...), kind=kLoop, calls=%fused_computation.107 | loop fusion | flops 9961470 | bytes 8929304 | tf_op jit(solution)/shard_map/reduce_sum | solution.py:120
  150.7 2.4 psum.51
  153.2 2.1 multiply_add_fusion.2
  155.4 2.1 collective-permute-start.11
  160.7 3.5 %multiply_reduce_fusion.1 = (f32[2]{0:T(128)S(1)}, f32[2,2,256,512]{3,2,1,0:T(8,128)}) fusion(f32[256,512]{1,0:T(8,128)S(1)} %copy-done.17, f32[2,2,256,512]{3,2,1,0:T(8,128)S(1)} %multiply_add_fusion.2, f32[256,512]{1,0:T(8,128)S(1)} %copy-done.11, f32[2,2,1,512]{3,2,1,0:T(1,128)S(1)} %collective-permute-done.12, f32[256,512]{1,0:T(8,128)S(1)} %copy-done.5, ...), kind=kLoop, calls=%fused_computation.105 | loop fusion | flops 9961470 | bytes 8929304 | tf_op jit(solution)/shard_map/reduce_sum | solution.py:120
  164.2 2.4 psum.52
  166.7 2.8 multiply_subtract_fusion
  169.5 2.1 collective-permute-start.13
  174.8 3.5 %multiply_reduce_fusion = (f32[2]{0:T(128)S(1)}, f32[2,2,256,512]{3,2,1,0:T(8,128)}) fusion(f32[256,512]{1,0:T(8,128)S(1)} %copy-done.18, f32[2,2,256,512]{3,2,1,0:T(8,128)S(1)} %multiply_subtract_fusion, f32[256,512]{1,0:T(8,128)S(1)} %copy-done.12, f32[2,2,1,512]{3,2,1,0:T(1,128)S(1)} %collective-permute-done.14, f32[256,512]{1,0:T(8,128)S(1)} %copy-done.6, ...), kind=kLoop, calls=%fused_computation.103 | loop fusion | flops 9961470 | bytes 8929304 | tf_op jit(solution)/shard_map/reduce_sum | solution.py:120
  178.3 2.4 psum.53
  180.8 2.8 multiply_add_fusion.1
  183.6 2.1 collective-permute-start.15
  188.9 2.5 fusion.36
  191.4 2.7 all-reduce.7
  194.0 3.1 %multiply_add_fusion = f32[2,2,256,512]{3,2,1,0:T(8,128)S(1)} fusion(f32[2,2,256,512]{3,2,1,0:T(8,128)} %copy-done, f32[2,2,256,512]{3,2,1,0:T(8,128)S(1)} %get-tuple-element.19, f32[2]{0:T(128)S(1)} %div.42, f32[2]{0:T(128)S(1)} %div.40, f32[2]{0:T(128)S(1)} %div.38, f32[2,2,256,512]{3,2,1,0:T(8,128)} %get-tuple-element.11, f32[2]{0:T(128)S(1)} %div.41), kind=kLoop, calls=%fused_computation.101 | loop fusion | flops 3670016 | bytes 8388640 | tf_op jit(solution)/shard_map/add | solution.py:133
  198.7 52.6 %all_to_all.67 = f32[2,2,256,512]{3,1,0,2:T(2,128)S(1)} all-to-all(f32[2,2,256,512]{3,1,0,2:T(2,128)S(1)} %copy.40), channel_id=1, replica_groups=mesh['groups'=2,'tm'=8,'rows'=2] {'tm'}, dimensions={2} | all-to-all | bytes 4194304 | tf_op jit(solution)/shard_map/all_to_all | solution.py:140
  257.2 3.8 %all-to-all-start.3 = ((f32[16,32,512]{2,1,0:T(8,128)}), f32[16,32,512]{2,1,0:T(8,128)S(1)}, u32[]{:S(2)}, u32[]{:S(2)}) async-start(f32[16,32,512]{2,1,0:T(8,128)} %bitcast.34), calls=%async_computation.3 | async-start | bytes 2097152 | tf_op jit(solution)/shard_map/all_to_all | solution.py:148
  261.5 25.0 %all-to-all-done.3 = f32[16,32,512]{2,1,0:T(8,128)S(1)} async-done(((f32[16,32,512]{2,1,0:T(8,128)}), f32[16,32,512]{2,1,0:T(8,128)S(1)}, u32[]{:S(2)}, u32[]{:S(2)}) %all-to-all-start.3) | async-done | bytes 1048608 | tf_op jit(solution)/shard_map/all_to_all | solution.py:148
  (128 shorter events, 43.3 us)
Async XLA Ops:
  0.6 14.3 %copy-start.23 = (f32[256,512]{1,0:T(8,128)S(1)}, f32[256,512]{1,0:T(8,128)}, u32[]{:S(2)}) copy-start(f32[256,512]{1,0:T(8,128)} %param.7) | copy-start | bytes 1572868
  1.4 13.6 %collective-permute-start.2 = (f32[1,512]{1,0:T(1,128)S(1)}, f32[1,512]{1,0:T(1,128)S(1)}, u32[]{:S(2)}, u32[]{:S(2)}) collective-permute-start(f32[1,512]{1,0:T(1,128)S(1)} %slice.228), channel_id=1, source_target_pairs={{1,0},{3,2},{5,4},{7,6},{9,8},{11,10},{13,12},{15,14},{17,16},{19,... | collective-permute-start | bytes 6152 | tf_op jit(solution)/shard_map/ppermute | solution.py:20
  3.5 24.0 %collective-permute-start.3 = (f32[2,1,512]{2,1,0:T(1,128)S(1)}, f32[2,1,512]{2,1,0:T(1,128)S(1)}, u32[]{:S(2)}, u32[]{:S(2)}) collective-permute-start(f32[2,1,512]{2,1,0:T(1,128)S(1)} %get-tuple-element.53), channel_id=1, source_target_pairs={{0,1},{2,3},{4,5},{6,7},{8,9},{10,11},{12,13},{14,15},{16,17},{18,... | collective-permute-start | bytes 12296 | tf_op jit(solution)/shard_map/ppermute | solution.py:17
  6.5 21.0 %collective-permute-start.4 = (f32[2,1,512]{2,1,0:T(1,128)S(1)}, f32[2,1,512]{2,1,0:T(1,128)S(1)}, u32[]{:S(2)}, u32[]{:S(2)}) collective-permute-start(f32[2,1,512]{2,1,0:T(1,128)S(1)} %get-tuple-element.54), channel_id=1, source_target_pairs={{1,0},{3,2},{5,4},{7,6},{9,8},{11,10},{13,12},{15,14},{17,16},{19,... | collective-permute-start | bytes 12296 | tf_op jit(solution)/shard_map/ppermute | solution.py:20
  9.9 17.5 %copy-start.25 = (f32[256,512]{1,0:T(8,128)S(1)}, f32[256,512]{1,0:T(8,128)}, u32[]{:S(2)}) copy-start(f32[256,512]{1,0:T(8,128)} %param.6) | copy-start | bytes 1572868
  9.9 17.5 %collective-permute-start = (f32[256,512]{1,0:T(8,128)}, f32[256,512]{1,0:T(8,128)S(1)}, u32[]{:S(2)}, u32[]{:S(2)}) collective-permute-start(f32[256,512]{1,0:T(8,128)} %get-tuple-element.51), channel_id=1, source_target_pairs={{0,2},{2,4},{4,6},{6,8},{8,10},{10,12},{12,14},{1,3},{3,5},{5,7},{... | collective-permute-start | bytes 1572872 | tf_op jit(solution)/shard_map/ppermute | solution.py:28
  15.1 3.6 %collective-permute-start.1 = (f32[1,512]{1,0:T(1,128)S(1)}, f32[1,512]{1,0:T(1,128)S(1)}, u32[]{:S(2)}, u32[]{:S(2)}) collective-permute-start(f32[1,512]{1,0:T(1,128)S(1)} %get-tuple-element.58), channel_id=1, source_target_pairs={{0,1},{2,3},{4,5},{6,7},{8,9},{10,11},{12,13},{14,15},{16,17},{18,... | collective-permute-start | bytes 6152 | tf_op jit(solution)/shard_map/ppermute | solution.py:17
  18.6 8.8 %copy-start.21 = (f32[2,256,512]{2,1,0:T(8,128)S(1)}, f32[2,256,512]{2,1,0:T(8,128)}, u32[]{:S(2)}) copy-start(f32[2,256,512]{2,1,0:T(8,128)} %param.4) | copy-start | bytes 3145732
  18.7 8.8 %copy-start.24 = (f32[2,256,512]{2,1,0:T(8,128)S(1)}, f32[2,256,512]{2,1,0:T(8,128)}, u32[]{:S(2)}) copy-start(f32[2,256,512]{2,1,0:T(8,128)} %param.5) | copy-start | bytes 3145732
  19.1 9.6 %copy-start.2 = (f32[256,512]{1,0:T(8,128)}, f32[256,512]{1,0:T(8,128)S(1)}, u32[]{:S(2)}) copy-start(f32[256,512]{1,0:T(8,128)S(1)} %get-tuple-element.22) | copy-start | bytes 1572868
  19.1 9.6 %copy-start.8 = (f32[256,512]{1,0:T(8,128)}, f32[256,512]{1,0:T(8,128)S(1)}, u32[]{:S(2)}) copy-start(f32[256,512]{1,0:T(8,128)S(1)} %get-tuple-element.23) | copy-start | bytes 1572868
  19.1 9.5 %copy-start.14 = (f32[256,512]{1,0:T(8,128)}, f32[256,512]{1,0:T(8,128)S(1)}, u32[]{:S(2)}) copy-start(f32[256,512]{1,0:T(8,128)S(1)} %get-tuple-element.24) | copy-start | bytes 1572868
  68.2 51.5 %all-to-all-start.1 = ((f32[2,16,32,512]{3,2,0,1:T(8,128)}), f32[2,16,32,512]{3,2,0,1:T(8,128)S(1)}, u32[]{:S(2)}, u32[]{:S(2)}) async-start(f32[2,16,32,512]{3,2,0,1:T(8,128)} %copy.35), calls=%async_computation.1 | async-start | bytes 4194304 | tf_op jit(solution)/shard_map/all_to_all | solution.py:100
  120.0 4.4 %copy-start.20 = (f32[2,2,8,32,512]{4,3,2,1,0:T(8,128)}, f32[2,2,8,32,512]{4,3,2,1,0:T(8,128)S(1)}, u32[]{:S(2)}) copy-start(f32[2,2,8,32,512]{4,3,2,1,0:T(8,128)S(1)} %copy.37) | copy-start | bytes 6291460
  120.0 3.4 %collective-permute-start.5 = (f32[2,2,1,512]{3,2,1,0:T(1,128)S(1)}, f32[2,2,1,512]{3,2,1,0:T(1,128)S(1)}, u32[]{:S(2)}, u32[]{:S(2)}) collective-permute-start(f32[2,2,1,512]{3,2,1,0:T(1,128)S(1)} %get-tuple-element.49), channel_id=1, source_target_pairs={{0,1},{2,3},{4,5},{6,7},{8,9},{10,11},{12,13},{14,15},{16,17},{18,... | collective-permute-start | bytes 24584 | tf_op jit(solution)/shard_map/ppermute | solution.py:17
  121.3 3.1 %collective-permute-start.6 = (f32[2,2,1,512]{3,2,1,0:T(1,128)S(1)}, f32[2,2,1,512]{3,2,1,0:T(1,128)S(1)}, u32[]{:S(2)}, u32[]{:S(2)}) collective-permute-start(f32[2,2,1,512]{3,2,1,0:T(1,128)S(1)} %get-tuple-element.50), channel_id=1, source_target_pairs={{1,0},{3,2},{5,4},{7,6},{9,8},{11,10},{13,12},{15,14},{17,16},{19,... | collective-permute-start | bytes 24584 | tf_op jit(solution)/shard_map/ppermute | solution.py:20
  127.1 4.7 %collective-permute-start.7 = (f32[2,2,1,512]{3,2,1,0:T(1,128)S(1)}, f32[2,2,1,512]{3,2,1,0:T(1,128)S(1)}, u32[]{:S(2)}, u32[]{:S(2)}) collective-permute-start(f32[2,2,1,512]{3,2,1,0:T(1,128)S(1)} %get-tuple-element.45), channel_id=1, source_target_pairs={{0,1},{2,3},{4,5},{6,7},{8,9},{10,11},{12,13},{14,15},{16,17},{18,... | collective-permute-start | bytes 24584 | tf_op jit(solution)/shard_map/ppermute | solution.py:17
  130.1 3.1 %collective-permute-start.8 = (f32[2,2,1,512]{3,2,1,0:T(1,128)S(1)}, f32[2,2,1,512]{3,2,1,0:T(1,128)S(1)}, u32[]{:S(2)}, u32[]{:S(2)}) collective-permute-start(f32[2,2,1,512]{3,2,1,0:T(1,128)S(1)} %get-tuple-element.46), channel_id=1, source_target_pairs={{1,0},{3,2},{5,4},{7,6},{9,8},{11,10},{13,12},{15,14},{17,16},{19,... | collective-permute-start | bytes 24584 | tf_op jit(solution)/shard_map/ppermute | solution.py:20
  141.8 5.4 %copy-start.1 = (f32[2,2,256,512]{3,2,1,0:T(8,128)}, f32[2,2,256,512]{3,2,1,0:T(8,128)S(1)}, u32[]{:S(2)}) copy-start(f32[2,2,256,512]{3,2,1,0:T(8,128)S(1)} %multiply_subtract_fusion.1) | copy-start | bytes 6291460
  141.9 3.8 %collective-permute-start.9 = (f32[2,2,1,512]{3,2,1,0:T(1,128)S(1)}, f32[2,2,1,512]{3,2,1,0:T(1,128)S(1)}, u32[]{:S(2)}, u32[]{:S(2)}) collective-permute-start(f32[2,2,1,512]{3,2,1,0:T(1,128)S(1)} %get-tuple-element.41), channel_id=1, source_target_pairs={{0,1},{2,3},{4,5},{6,7},{8,9},{10,11},{12,13},{14,15},{16,17},{18,... | collective-permute-start | bytes 24584 | tf_op jit(solution)/shard_map/ppermute | solution.py:17
  144.0 3.2 %copy-start.4 = (f32[256,512]{1,0:T(8,128)S(1)}, f32[256,512]{1,0:T(8,128)}, u32[]{:S(2)}) copy-start(f32[256,512]{1,0:T(8,128)} %copy-done.2) | copy-start | bytes 1572868
  144.0 3.2 %collective-permute-start.10 = (f32[2,2,1,512]{3,2,1,0:T(1,128)S(1)}, f32[2,2,1,512]{3,2,1,0:T(1,128)S(1)}, u32[]{:S(2)}, u32[]{:S(2)}) collective-permute-start(f32[2,2,1,512]{3,2,1,0:T(1,128)S(1)} %get-tuple-element.42), channel_id=1, source_target_pairs={{1,0},{3,2},{5,4},{7,6},{9,8},{11,10},{13,12},{15,14},{17,16},{19,... | collective-permute-start | bytes 24584 | tf_op jit(solution)/shard_map/ppermute | solution.py:20
  155.3 5.3 %copy-start = (f32[2,2,256,512]{3,2,1,0:T(8,128)}, f32[2,2,256,512]{3,2,1,0:T(8,128)S(1)}, u32[]{:S(2)}) copy-start(f32[2,2,256,512]{3,2,1,0:T(8,128)S(1)} %multiply_add_fusion.2) | copy-start | bytes 6291460
  155.4 3.8 %collective-permute-start.11 = (f32[2,2,1,512]{3,2,1,0:T(1,128)S(1)}, f32[2,2,1,512]{3,2,1,0:T(1,128)S(1)}, u32[]{:S(2)}, u32[]{:S(2)}) collective-permute-start(f32[2,2,1,512]{3,2,1,0:T(1,128)S(1)} %get-tuple-element.37), channel_id=1, source_target_pairs={{0,1},{2,3},{4,5},{6,7},{8,9},{10,11},{12,13},{14,15},{16,17},{18,... | collective-permute-start | bytes 24584 | tf_op jit(solution)/shard_map/ppermute | solution.py:17
  157.4 3.2 %copy-start.5 = (f32[256,512]{1,0:T(8,128)S(1)}, f32[256,512]{1,0:T(8,128)}, u32[]{:S(2)}) copy-start(f32[256,512]{1,0:T(8,128)} %copy-done.2) | copy-start | bytes 1572868
  157.5 3.2 %collective-permute-start.12 = (f32[2,2,1,512]{3,2,1,0:T(1,128)S(1)}, f32[2,2,1,512]{3,2,1,0:T(1,128)S(1)}, u32[]{:S(2)}, u32[]{:S(2)}) collective-permute-start(f32[2,2,1,512]{3,2,1,0:T(1,128)S(1)} %get-tuple-element.38), channel_id=1, source_target_pairs={{1,0},{3,2},{5,4},{7,6},{9,8},{11,10},{13,12},{15,14},{17,16},{19,... | collective-permute-start | bytes 24584 | tf_op jit(solution)/shard_map/ppermute | solution.py:20
  169.5 3.8 %collective-permute-start.13 = (f32[2,2,1,512]{3,2,1,0:T(1,128)S(1)}, f32[2,2,1,512]{3,2,1,0:T(1,128)S(1)}, u32[]{:S(2)}, u32[]{:S(2)}) collective-permute-start(f32[2,2,1,512]{3,2,1,0:T(1,128)S(1)} %get-tuple-element.33), channel_id=1, source_target_pairs={{0,1},{2,3},{4,5},{6,7},{8,9},{10,11},{12,13},{14,15},{16,17},{18,... | collective-permute-start | bytes 24584 | tf_op jit(solution)/shard_map/ppermute | solution.py:17
  171.6 3.2 %collective-permute-start.14 = (f32[2,2,1,512]{3,2,1,0:T(1,128)S(1)}, f32[2,2,1,512]{3,2,1,0:T(1,128)S(1)}, u32[]{:S(2)}, u32[]{:S(2)}) collective-permute-start(f32[2,2,1,512]{3,2,1,0:T(1,128)S(1)} %get-tuple-element.34), channel_id=1, source_target_pairs={{1,0},{3,2},{5,4},{7,6},{9,8},{11,10},{13,12},{15,14},{17,16},{19,... | collective-permute-start | bytes 24584 | tf_op jit(solution)/shard_map/ppermute | solution.py:20
  183.6 3.8 %collective-permute-start.15 = (f32[2,2,1,512]{3,2,1,0:T(1,128)S(1)}, f32[2,2,1,512]{3,2,1,0:T(1,128)S(1)}, u32[]{:S(2)}, u32[]{:S(2)}) collective-permute-start(f32[2,2,1,512]{3,2,1,0:T(1,128)S(1)} %get-tuple-element.29), channel_id=1, source_target_pairs={{0,1},{2,3},{4,5},{6,7},{8,9},{10,11},{12,13},{14,15},{16,17},{18,... | collective-permute-start | bytes 24584 | tf_op jit(solution)/shard_map/ppermute | solution.py:17
  185.7 3.2 %collective-permute-start.16 = (f32[2,2,1,512]{3,2,1,0:T(1,128)S(1)}, f32[2,2,1,512]{3,2,1,0:T(1,128)S(1)}, u32[]{:S(2)}, u32[]{:S(2)}) collective-permute-start(f32[2,2,1,512]{3,2,1,0:T(1,128)S(1)} %get-tuple-element.30), channel_id=1, source_target_pairs={{1,0},{3,2},{5,4},{7,6},{9,8},{11,10},{13,12},{15,14},{17,16},{19,... | collective-permute-start | bytes 24584 | tf_op jit(solution)/shard_map/ppermute | solution.py:20
  257.2 29.4 %copy-start.22 = (f32[2,256,512]{2,1,0:T(8,128)S(1)}, f32[2,256,512]{2,1,0:T(8,128)}, u32[]{:S(2)}) copy-start(f32[2,256,512]{2,1,0:T(8,128)} %param.4) | copy-start | bytes 3145732
  257.2 29.3 %all-to-all-start.3 = ((f32[16,32,512]{2,1,0:T(8,128)}), f32[16,32,512]{2,1,0:T(8,128)S(1)}, u32[]{:S(2)}, u32[]{:S(2)}) async-start(f32[16,32,512]{2,1,0:T(8,128)} %bitcast.34), calls=%async_computation.3 | async-start | bytes 2097152 | tf_op jit(solution)/shard_map/all_to_all | solution.py:148
  (13 other events, 36.0 us)
where the time goes:
time: 289 us; the launch traced here: 288 us
  blocking collectives  97.5 us (34%)
  waiting for transfers between devices  90.2 us (31%)
  starting transfers between devices  41.9 us (14%)
  other arithmetic  38 us (13%)
  local copies, waits for them, and re-layouts  13.8 us (5%)
  matrix products  5.1 us (2%)
    all_to_all x1, blocking collectives, shards(): lax.all_to_all(solution, 'tm', split_axis=2, concat_axis=1, tiled=True)  52.6 us
    all_to_all x1, waiting for transfers between devices, shards(): lax.all_to_all(spectrum, 'tm', split_axis=1, concat_axis=2, tiled=True)  47.8 us
    all_to_all x1, blocking collectives, shards(): lax.all_to_all(scaled, 'tm', split_axis=1, concat_axis=0, tiled=True)  32.5 us
    all_to_all x1, waiting for transfers between devices, shards(): lax.all_to_all(correction, 'tm', split_axis=0, concat_axis=1, tiled=True)  25 us
    reduce_sum x6, other arithmetic, freq_norm(): return jnp.sum(values * values, axis=(0, 2, 3))  19 us
    ppermute x8, starting transfers between devices, extended(): lax.ppermute(lax.slice_in_dim(block, block.shape[dim] - width, None, axis...  18.4 us
    psum x5, blocking collectives, reduce_sums(): return lax.psum(values, 'rows')  12.4 us
    ppermute x8, starting transfers between devices, extended(): lax.ppermute(lax.slice_in_dim(block, 0, width, axis=dim), axis, backward)  11 us
  transfers between devices with their start and end apart: 19, of which 10 were waited for; matrix products, arithmetic and copies ran while one was open for 2% of the time, Pallas kernels for 0%

commit v1 on v0

--- a/solution.py
+++ b/solution.py
@@ -145,7 +145,16 @@
         jnp.sin(inverse_angles) / length, flat_imag
     )
     correction = correction.reshape(length, slab_rows, columns_dev)
-    own_steps = lax.all_to_all(correction, "tm", split_axis=0, concat_axis=1, tiled=True)
+    finish_field_all = lambda block_here, dev_axis: jnp.concatenate(
+        lax.all_to_all(
+            jnp.stack(jnp.split(block_here, lax.axis_size(dev_axis), axis=0), axis=0),
+            dev_axis,
+            0,
+            0,
+        ),
+        axis=1,
+    )
+    own_steps = finish_field_all(correction, "tm")
     updated = iterate + own_steps / growth[:, None, None]
     return (updated, residual_rms)
 

time: 289 us -> 293 us (1.014)
  local copies, waits for them, and re-layouts: 13.8 us -> 18 us
    unnamed x55 -> x61, local copies, waits for them, and re-layouts: 3.09 us -> 6.27 us
where the time goes in v1:
time: 293 us; the launch traced here: 292 us
  blocking collectives  97.5 us (33%)
  waiting for transfers between devices  90.2 us (31%)
  starting transfers between devices  41.8 us (14%)
  other arithmetic  38 us (13%)
  local copies, waits for them, and re-layouts  18 us (6%)
  matrix products  5.1 us (2%)
    all_to_all x1, blocking collectives, shards(): lax.all_to_all(solution, 'tm', split_axis=2, concat_axis=1, tiled=True)  52.6 us
    all_to_all x1, waiting for transfers between devices, shards(): lax.all_to_all(spectrum, 'tm', split_axis=1, concat_axis=2, tiled=True)  47.7 us
    all_to_all x1, blocking collectives, shards(): lax.all_to_all(scaled, 'tm', split_axis=1, concat_axis=0, tiled=True)  32.5 us
    all_to_all x1, waiting for transfers between devices, shards(): lax.all_to_all(jnp.stack(jnp.split(block_here, lax.axis_size(dev_axis), a...  25 us
    reduce_sum x6, other arithmetic, freq_norm(): return jnp.sum(values * values, axis=(0, 2, 3))  19 us
    ppermute x8, starting transfers between devices, extended(): lax.ppermute(lax.slice_in_dim(block, block.shape[dim] - width, None, axis...  18.4 us
    psum x5, blocking collectives, reduce_sums(): return lax.psum(values, 'rows')  12.4 us
    ppermute x8, starting transfers between devices, extended(): lax.ppermute(lax.slice_in_dim(block, 0, width, axis=dim), axis, backward)  11 us
  transfers between devices with their start and end apart: 19, of which 10 were waited for; matrix products, arithmetic and copies ran while one was open for 2% of the time, Pallas kernels for 0%

profile of v1, /device:TPU:0, one launch (start us, length us, event | category | flops | bytes accessed | tf_op | source)
XLA Modules:
  0.0 292.1 jit_solution(7274672574727007025)
XLA Ops:
  3.5 3.0 %collective-permute-start.3 = (f32[2,1,512]{2,1,0:T(1,128)S(1)}, f32[2,1,512]{2,1,0:T(1,128)S(1)}, u32[]{:S(2)}, u32[]{:S(2)}) collective-permute-start(f32[2,1,512]{2,1,0:T(1,128)S(1)} %get-tuple-element.61), channel_id=1, source_target_pairs={{0,1},{2,3},{4,5},{6,7},{8,9},{10,11},{12,13},{14,15},{16,17},{18,... | collective-permute-start | bytes 12296 | tf_op jit(solution)/shard_map/ppermute | solution.py:17
  9.9 5.1 %collective-permute-start = (f32[256,512]{1,0:T(8,128)}, f32[256,512]{1,0:T(8,128)S(1)}, u32[]{:S(2)}, u32[]{:S(2)}) collective-permute-start(f32[256,512]{1,0:T(8,128)} %get-tuple-element.59), channel_id=1, source_target_pairs={{0,2},{2,4},{4,6},{6,8},{8,10},{10,12},{12,14},{1,3},{3,5},{5,7},{... | collective-permute-start | bytes 1572872 | tf_op jit(solution)/shard_map/ppermute | solution.py:28
  15.1 2.7 collective-permute-start.1
  19.1 8.3 %collective-permute-done = f32[256,512]{1,0:T(8,128)S(1)} collective-permute-done((f32[256,512]{1,0:T(8,128)}, f32[256,512]{1,0:T(8,128)S(1)}, u32[]{:S(2)}, u32[]{:S(2)}) %collective-permute-start) | collective-permute-done | bytes 524320 | tf_op jit(solution)/shard_map/ppermute | solution.py:28
  29.6 32.5 %all_to_all.53 = f32[2,256,512]{2,0,1:T(2,128)S(1)} all-to-all(f32[2,256,512]{2,0,1:T(2,128)S(1)} %copy.31), channel_id=1, replica_groups=mesh['groups'=2,'tm'=8,'rows'=2] {'tm'}, dimensions={1} | all-to-all | bytes 2097152 | tf_op jit(solution)/shard_map/all_to_all | solution.py:92
  65.7 2.6 copy.35
  68.3 3.6 %all-to-all-start.1 = ((f32[2,16,32,512]{3,2,0,1:T(8,128)}), f32[2,16,32,512]{3,2,0,1:T(8,128)S(1)}, u32[]{:S(2)}, u32[]{:S(2)}) async-start(f32[2,16,32,512]{3,2,0,1:T(8,128)} %copy.35), calls=%async_computation.1 | async-start | bytes 4194304 | tf_op jit(solution)/shard_map/all_to_all | solution.py:100
  72.0 47.7 %all-to-all-done.1 = f32[2,16,32,512]{3,2,0,1:T(8,128)S(1)} async-done(((f32[2,16,32,512]{3,2,0,1:T(8,128)}), f32[2,16,32,512]{3,2,0,1:T(8,128)S(1)}, u32[]{:S(2)}, u32[]{:S(2)}) %all-to-all-start.1) | async-done | bytes 2097184 | tf_op jit(solution)/shard_map/all_to_all | solution.py:100
  124.6 2.5 multiply_reduce_fusion.4
  127.1 3.0 %collective-permute-start.7 = (f32[2,2,1,512]{3,2,1,0:T(1,128)S(1)}, f32[2,2,1,512]{3,2,1,0:T(1,128)S(1)}, u32[]{:S(2)}, u32[]{:S(2)}) collective-permute-start(f32[2,2,1,512]{3,2,1,0:T(1,128)S(1)} %get-tuple-element.45), channel_id=1, source_target_pairs={{0,1},{2,3},{4,5},{6,7},{8,9},{10,11},{12,13},{14,15},{16,17},{18,... | collective-permute-start | bytes 24584 | tf_op jit(solution)/shard_map/ppermute | solution.py:17
  133.2 3.4 %multiply_reduce_fusion.3 = (f32[2]{0:T(128)S(1)}, f32[2,2,256,512]{3,2,1,0:T(8,128)}) fusion(f32[256,512]{1,0:T(8,128)S(1)} %copy-done.15, f32[2,2,256,512]{3,2,1,0:T(8,128)S(1)} %get-tuple-element.19, f32[256,512]{1,0:T(8,128)S(1)} %copy-done.9, f32[2,2,1,512]{3,2,1,0:T(1,128)S(1)} %collective-permute-done.8, f32[256,512]{1,0:T(8,128)S(1)} %copy-done.3, ...), kind=kLoop, calls=%fused_computation.109 | loop fusion | flops 9961470 | bytes 8929304 | tf_op jit(solution)/shard_map/reduce_sum | solution.py:120
  136.6 2.4 all-reduce.8
  139.1 2.8 multiply_subtract_fusion.1
  141.9 2.1 collective-permute-start.9
  147.2 3.5 %multiply_reduce_fusion.2 = (f32[2]{0:T(128)S(1)}, f32[2,2,256,512]{3,2,1,0:T(8,128)}) fusion(f32[256,512]{1,0:T(8,128)S(1)} %copy-done.16, f32[2,2,256,512]{3,2,1,0:T(8,128)S(1)} %multiply_subtract_fusion.1, f32[256,512]{1,0:T(8,128)S(1)} %copy-done.10, f32[2,2,1,512]{3,2,1,0:T(1,128)S(1)} %collective-permute-done.10, f32[256,512]{1,0:T(8,128)S(1)} %copy-done.4, ...), kind=kLoop, calls=%fused_computation.107 | loop fusion | flops 9961470 | bytes 8929304 | tf_op jit(solution)/shard_map/reduce_sum | solution.py:120
  150.7 2.4 psum.51
  153.2 2.1 multiply_add_fusion.2
  155.4 2.1 collective-permute-start.11
  160.7 3.5 %multiply_reduce_fusion.1 = (f32[2]{0:T(128)S(1)}, f32[2,2,256,512]{3,2,1,0:T(8,128)}) fusion(f32[256,512]{1,0:T(8,128)S(1)} %copy-done.17, f32[2,2,256,512]{3,2,1,0:T(8,128)S(1)} %multiply_add_fusion.2, f32[256,512]{1,0:T(8,128)S(1)} %copy-done.11, f32[2,2,1,512]{3,2,1,0:T(1,128)S(1)} %collective-permute-done.12, f32[256,512]{1,0:T(8,128)S(1)} %copy-done.5, ...), kind=kLoop, calls=%fused_computation.105 | loop fusion | flops 9961470 | bytes 8929304 | tf_op jit(solution)/shard_map/reduce_sum | solution.py:120
  164.3 2.4 psum.52
  166.7 2.8 multiply_subtract_fusion
  169.5 2.1 collective-permute-start.13
  174.8 3.5 %multiply_reduce_fusion = (f32[2]{0:T(128)S(1)}, f32[2,2,256,512]{3,2,1,0:T(8,128)}) fusion(f32[256,512]{1,0:T(8,128)S(1)} %copy-done.18, f32[2,2,256,512]{3,2,1,0:T(8,128)S(1)} %multiply_subtract_fusion, f32[256,512]{1,0:T(8,128)S(1)} %copy-done.12, f32[2,2,1,512]{3,2,1,0:T(1,128)S(1)} %collective-permute-done.14, f32[256,512]{1,0:T(8,128)S(1)} %copy-done.6, ...), kind=kLoop, calls=%fused_computation.103 | loop fusion | flops 9961470 | bytes 8929304 | tf_op jit(solution)/shard_map/reduce_sum | solution.py:120
  178.3 2.4 psum.53
  180.8 2.8 multiply_add_fusion.1
  183.6 2.1 collective-permute-start.15
  188.9 2.5 fusion.36
  191.4 2.7 all-reduce.7
  194.1 3.1 %multiply_add_fusion = f32[2,2,256,512]{3,2,1,0:T(8,128)S(1)} fusion(f32[2,2,256,512]{3,2,1,0:T(8,128)} %copy-done, f32[2,2,256,512]{3,2,1,0:T(8,128)S(1)} %get-tuple-element.19, f32[2]{0:T(128)S(1)} %div.42, f32[2]{0:T(128)S(1)} %div.40, f32[2]{0:T(128)S(1)} %div.38, f32[2,2,256,512]{3,2,1,0:T(8,128)} %get-tuple-element.11, f32[2]{0:T(128)S(1)} %div.41), kind=kLoop, calls=%fused_computation.101 | loop fusion | flops 3670016 | bytes 8388640 | tf_op jit(solution)/shard_map/add | solution.py:133
  198.8 52.6 %all_to_all.54 = f32[2,2,256,512]{3,1,0,2:T(2,128)S(1)} all-to-all(f32[2,2,256,512]{3,1,0,2:T(2,128)S(1)} %copy.40), channel_id=1, replica_groups=mesh['groups'=2,'tm'=8,'rows'=2] {'tm'}, dimensions={2} | all-to-all | bytes 4194304 | tf_op jit(solution)/shard_map/all_to_all | solution.py:140
  261.4 3.8 %all-to-all-start.3 = ((f32[8,2,32,512]{3,2,1,0:T(8,128)}), f32[8,2,32,512]{3,2,1,0:T(8,128)S(1)}, u32[]{:S(2)}, u32[]{:S(2)}) async-start(f32[8,2,32,512]{3,2,1,0:T(8,128)} %bitcast_dynamic-update-slice_fusion), calls=%async_computation.3 | async-start | bytes 2097152 | tf_op jit(solution)/shard_map/all_to_all | solution.py:149
  265.7 25.0 %all-to-all-done.3 = f32[8,2,32,512]{3,2,1,0:T(8,128)S(1)} async-done(((f32[8,2,32,512]{3,2,1,0:T(8,128)}), f32[8,2,32,512]{3,2,1,0:T(8,128)S(1)}, u32[]{:S(2)}, u32[]{:S(2)}) %all-to-all-start.3) | async-done | bytes 1048608 | tf_op jit(solution)/shard_map/all_to_all | solution.py:149
  (136 shorter events, 47.5 us)
Async XLA Ops:
  0.6 14.3 %copy-start.23 = (f32[256,512]{1,0:T(8,128)S(1)}, f32[256,512]{1,0:T(8,128)}, u32[]{:S(2)}) copy-start(f32[256,512]{1,0:T(8,128)} %param.7) | copy-start | bytes 1572868
  1.4 13.6 %collective-permute-start.2 = (f32[1,512]{1,0:T(1,128)S(1)}, f32[1,512]{1,0:T(1,128)S(1)}, u32[]{:S(2)}, u32[]{:S(2)}) collective-permute-start(f32[1,512]{1,0:T(1,128)S(1)} %slice.236), channel_id=1, source_target_pairs={{1,0},{3,2},{5,4},{7,6},{9,8},{11,10},{13,12},{15,14},{17,16},{19,... | collective-permute-start | bytes 6152 | tf_op jit(solution)/shard_map/ppermute | solution.py:20
  3.5 24.0 %collective-permute-start.3 = (f32[2,1,512]{2,1,0:T(1,128)S(1)}, f32[2,1,512]{2,1,0:T(1,128)S(1)}, u32[]{:S(2)}, u32[]{:S(2)}) collective-permute-start(f32[2,1,512]{2,1,0:T(1,128)S(1)} %get-tuple-element.61), channel_id=1, source_target_pairs={{0,1},{2,3},{4,5},{6,7},{8,9},{10,11},{12,13},{14,15},{16,17},{18,... | collective-permute-start | bytes 12296 | tf_op jit(solution)/shard_map/ppermute | solution.py:17
  6.5 21.0 %collective-permute-start.4 = (f32[2,1,512]{2,1,0:T(1,128)S(1)}, f32[2,1,512]{2,1,0:T(1,128)S(1)}, u32[]{:S(2)}, u32[]{:S(2)}) collective-permute-start(f32[2,1,512]{2,1,0:T(1,128)S(1)} %get-tuple-element.62), channel_id=1, source_target_pairs={{1,0},{3,2},{5,4},{7,6},{9,8},{11,10},{13,12},{15,14},{17,16},{19,... | collective-permute-start | bytes 12296 | tf_op jit(solution)/shard_map/ppermute | solution.py:20
  9.9 17.5 %copy-start.25 = (f32[256,512]{1,0:T(8,128)S(1)}, f32[256,512]{1,0:T(8,128)}, u32[]{:S(2)}) copy-start(f32[256,512]{1,0:T(8,128)} %param.6) | copy-start | bytes 1572868
  9.9 17.5 %collective-permute-start = (f32[256,512]{1,0:T(8,128)}, f32[256,512]{1,0:T(8,128)S(1)}, u32[]{:S(2)}, u32[]{:S(2)}) collective-permute-start(f32[256,512]{1,0:T(8,128)} %get-tuple-element.59), channel_id=1, source_target_pairs={{0,2},{2,4},{4,6},{6,8},{8,10},{10,12},{12,14},{1,3},{3,5},{5,7},{... | collective-permute-start | bytes 1572872 | tf_op jit(solution)/shard_map/ppermute | solution.py:28
  15.1 3.6 %collective-permute-start.1 = (f32[1,512]{1,0:T(1,128)S(1)}, f32[1,512]{1,0:T(1,128)S(1)}, u32[]{:S(2)}, u32[]{:S(2)}) collective-permute-start(f32[1,512]{1,0:T(1,128)S(1)} %get-tuple-element.66), channel_id=1, source_target_pairs={{0,1},{2,3},{4,5},{6,7},{8,9},{10,11},{12,13},{14,15},{16,17},{18,... | collective-permute-start | bytes 6152 | tf_op jit(solution)/shard_map/ppermute | solution.py:17
  18.7 8.8 %copy-start.21 = (f32[2,256,512]{2,1,0:T(8,128)S(1)}, f32[2,256,512]{2,1,0:T(8,128)}, u32[]{:S(2)}) copy-start(f32[2,256,512]{2,1,0:T(8,128)} %param.4) | copy-start | bytes 3145732
  18.7 8.8 %copy-start.24 = (f32[2,256,512]{2,1,0:T(8,128)S(1)}, f32[2,256,512]{2,1,0:T(8,128)}, u32[]{:S(2)}) copy-start(f32[2,256,512]{2,1,0:T(8,128)} %param.5) | copy-start | bytes 3145732
  19.1 9.6 %copy-start.2 = (f32[256,512]{1,0:T(8,128)}, f32[256,512]{1,0:T(8,128)S(1)}, u32[]{:S(2)}) copy-start(f32[256,512]{1,0:T(8,128)S(1)} %get-tuple-element.22) | copy-start | bytes 1572868
  19.1 9.6 %copy-start.8 = (f32[256,512]{1,0:T(8,128)}, f32[256,512]{1,0:T(8,128)S(1)}, u32[]{:S(2)}) copy-start(f32[256,512]{1,0:T(8,128)S(1)} %get-tuple-element.23) | copy-start | bytes 1572868
  19.1 9.5 %copy-start.14 = (f32[256,512]{1,0:T(8,128)}, f32[256,512]{1,0:T(8,128)S(1)}, u32[]{:S(2)}) copy-start(f32[256,512]{1,0:T(8,128)S(1)} %get-tuple-element.24) | copy-start | bytes 1572868
  68.3 51.5 %all-to-all-start.1 = ((f32[2,16,32,512]{3,2,0,1:T(8,128)}), f32[2,16,32,512]{3,2,0,1:T(8,128)S(1)}, u32[]{:S(2)}, u32[]{:S(2)}) async-start(f32[2,16,32,512]{3,2,0,1:T(8,128)} %copy.35), calls=%async_computation.1 | async-start | bytes 4194304 | tf_op jit(solution)/shard_map/all_to_all | solution.py:100
  120.0 4.4 %copy-start.20 = (f32[2,2,8,32,512]{4,3,2,1,0:T(8,128)}, f32[2,2,8,32,512]{4,3,2,1,0:T(8,128)S(1)}, u32[]{:S(2)}) copy-start(f32[2,2,8,32,512]{4,3,2,1,0:T(8,128)S(1)} %copy.37) | copy-start | bytes 6291460
  120.1 3.4 %collective-permute-start.5 = (f32[2,2,1,512]{3,2,1,0:T(1,128)S(1)}, f32[2,2,1,512]{3,2,1,0:T(1,128)S(1)}, u32[]{:S(2)}, u32[]{:S(2)}) collective-permute-start(f32[2,2,1,512]{3,2,1,0:T(1,128)S(1)} %get-tuple-element.49), channel_id=1, source_target_pairs={{0,1},{2,3},{4,5},{6,7},{8,9},{10,11},{12,13},{14,15},{16,17},{18,... | collective-permute-start | bytes 24584 | tf_op jit(solution)/shard_map/ppermute | solution.py:17
  121.4 3.1 %collective-permute-start.6 = (f32[2,2,1,512]{3,2,1,0:T(1,128)S(1)}, f32[2,2,1,512]{3,2,1,0:T(1,128)S(1)}, u32[]{:S(2)}, u32[]{:S(2)}) collective-permute-start(f32[2,2,1,512]{3,2,1,0:T(1,128)S(1)} %get-tuple-element.50), channel_id=1, source_target_pairs={{1,0},{3,2},{5,4},{7,6},{9,8},{11,10},{13,12},{15,14},{17,16},{19,... | collective-permute-start | bytes 24584 | tf_op jit(solution)/shard_map/ppermute | solution.py:20
  127.1 4.7 %collective-permute-start.7 = (f32[2,2,1,512]{3,2,1,0:T(1,128)S(1)}, f32[2,2,1,512]{3,2,1,0:T(1,128)S(1)}, u32[]{:S(2)}, u32[]{:S(2)}) collective-permute-start(f32[2,2,1,512]{3,2,1,0:T(1,128)S(1)} %get-tuple-element.45), channel_id=1, source_target_pairs={{0,1},{2,3},{4,5},{6,7},{8,9},{10,11},{12,13},{14,15},{16,17},{18,... | collective-permute-start | bytes 24584 | tf_op jit(solution)/shard_map/ppermute | solution.py:17
  130.2 3.1 %collective-permute-start.8 = (f32[2,2,1,512]{3,2,1,0:T(1,128)S(1)}, f32[2,2,1,512]{3,2,1,0:T(1,128)S(1)}, u32[]{:S(2)}, u32[]{:S(2)}) collective-permute-start(f32[2,2,1,512]{3,2,1,0:T(1,128)S(1)} %get-tuple-element.46), channel_id=1, source_target_pairs={{1,0},{3,2},{5,4},{7,6},{9,8},{11,10},{13,12},{15,14},{17,16},{19,... | collective-permute-start | bytes 24584 | tf_op jit(solution)/shard_map/ppermute | solution.py:20
  141.8 5.4 %copy-start.1 = (f32[2,2,256,512]{3,2,1,0:T(8,128)}, f32[2,2,256,512]{3,2,1,0:T(8,128)S(1)}, u32[]{:S(2)}) copy-start(f32[2,2,256,512]{3,2,1,0:T(8,128)S(1)} %multiply_subtract_fusion.1) | copy-start | bytes 6291460
  141.9 3.8 %collective-permute-start.9 = (f32[2,2,1,512]{3,2,1,0:T(1,128)S(1)}, f32[2,2,1,512]{3,2,1,0:T(1,128)S(1)}, u32[]{:S(2)}, u32[]{:S(2)}) collective-permute-start(f32[2,2,1,512]{3,2,1,0:T(1,128)S(1)} %get-tuple-element.41), channel_id=1, source_target_pairs={{0,1},{2,3},{4,5},{6,7},{8,9},{10,11},{12,13},{14,15},{16,17},{18,... | collective-permute-start | bytes 24584 | tf_op jit(solution)/shard_map/ppermute | solution.py:17
  144.0 3.2 %copy-start.4 = (f32[256,512]{1,0:T(8,128)S(1)}, f32[256,512]{1,0:T(8,128)}, u32[]{:S(2)}) copy-start(f32[256,512]{1,0:T(8,128)} %copy-done.2) | copy-start | bytes 1572868
  144.0 3.2 %collective-permute-start.10 = (f32[2,2,1,512]{3,2,1,0:T(1,128)S(1)}, f32[2,2,1,512]{3,2,1,0:T(1,128)S(1)}, u32[]{:S(2)}, u32[]{:S(2)}) collective-permute-start(f32[2,2,1,512]{3,2,1,0:T(1,128)S(1)} %get-tuple-element.42), channel_id=1, source_target_pairs={{1,0},{3,2},{5,4},{7,6},{9,8},{11,10},{13,12},{15,14},{17,16},{19,... | collective-permute-start | bytes 24584 | tf_op jit(solution)/shard_map/ppermute | solution.py:20
  155.3 5.3 %copy-start = (f32[2,2,256,512]{3,2,1,0:T(8,128)}, f32[2,2,256,512]{3,2,1,0:T(8,128)S(1)}, u32[]{:S(2)}) copy-start(f32[2,2,256,512]{3,2,1,0:T(8,128)S(1)} %multiply_add_fusion.2) | copy-start | bytes 6291460
  155.4 3.8 %collective-permute-start.11 = (f32[2,2,1,512]{3,2,1,0:T(1,128)S(1)}, f32[2,2,1,512]{3,2,1,0:T(1,128)S(1)}, u32[]{:S(2)}, u32[]{:S(2)}) collective-permute-start(f32[2,2,1,512]{3,2,1,0:T(1,128)S(1)} %get-tuple-element.37), channel_id=1, source_target_pairs={{0,1},{2,3},{4,5},{6,7},{8,9},{10,11},{12,13},{14,15},{16,17},{18,... | collective-permute-start | bytes 24584 | tf_op jit(solution)/shard_map/ppermute | solution.py:17
  157.5 3.2 %copy-start.5 = (f32[256,512]{1,0:T(8,128)S(1)}, f32[256,512]{1,0:T(8,128)}, u32[]{:S(2)}) copy-start(f32[256,512]{1,0:T(8,128)} %copy-done.2) | copy-start | bytes 1572868
  157.5 3.2 %collective-permute-start.12 = (f32[2,2,1,512]{3,2,1,0:T(1,128)S(1)}, f32[2,2,1,512]{3,2,1,0:T(1,128)S(1)}, u32[]{:S(2)}, u32[]{:S(2)}) collective-permute-start(f32[2,2,1,512]{3,2,1,0:T(1,128)S(1)} %get-tuple-element.38), channel_id=1, source_target_pairs={{1,0},{3,2},{5,4},{7,6},{9,8},{11,10},{13,12},{15,14},{17,16},{19,... | collective-permute-start | bytes 24584 | tf_op jit(solution)/shard_map/ppermute | solution.py:20
  169.5 3.8 %collective-permute-start.13 = (f32[2,2,1,512]{3,2,1,0:T(1,128)S(1)}, f32[2,2,1,512]{3,2,1,0:T(1,128)S(1)}, u32[]{:S(2)}, u32[]{:S(2)}) collective-permute-start(f32[2,2,1,512]{3,2,1,0:T(1,128)S(1)} %get-tuple-element.33), channel_id=1, source_target_pairs={{0,1},{2,3},{4,5},{6,7},{8,9},{10,11},{12,13},{14,15},{16,17},{18,... | collective-permute-start | bytes 24584 | tf_op jit(solution)/shard_map/ppermute | solution.py:17
  171.6 3.2 %collective-permute-start.14 = (f32[2,2,1,512]{3,2,1,0:T(1,128)S(1)}, f32[2,2,1,512]{3,2,1,0:T(1,128)S(1)}, u32[]{:S(2)}, u32[]{:S(2)}) collective-permute-start(f32[2,2,1,512]{3,2,1,0:T(1,128)S(1)} %get-tuple-element.34), channel_id=1, source_target_pairs={{1,0},{3,2},{5,4},{7,6},{9,8},{11,10},{13,12},{15,14},{17,16},{19,... | collective-permute-start | bytes 24584 | tf_op jit(solution)/shard_map/ppermute | solution.py:20
  183.6 3.8 %collective-permute-start.15 = (f32[2,2,1,512]{3,2,1,0:T(1,128)S(1)}, f32[2,2,1,512]{3,2,1,0:T(1,128)S(1)}, u32[]{:S(2)}, u32[]{:S(2)}) collective-permute-start(f32[2,2,1,512]{3,2,1,0:T(1,128)S(1)} %get-tuple-element.29), channel_id=1, source_target_pairs={{0,1},{2,3},{4,5},{6,7},{8,9},{10,11},{12,13},{14,15},{16,17},{18,... | collective-permute-start | bytes 24584 | tf_op jit(solution)/shard_map/ppermute | solution.py:17
  185.7 3.2 %collective-permute-start.16 = (f32[2,2,1,512]{3,2,1,0:T(1,128)S(1)}, f32[2,2,1,512]{3,2,1,0:T(1,128)S(1)}, u32[]{:S(2)}, u32[]{:S(2)}) collective-permute-start(f32[2,2,1,512]{3,2,1,0:T(1,128)S(1)} %get-tuple-element.30), channel_id=1, source_target_pairs={{1,0},{3,2},{5,4},{7,6},{9,8},{11,10},{13,12},{15,14},{17,16},{19,... | collective-permute-start | bytes 24584 | tf_op jit(solution)/shard_map/ppermute | solution.py:20
  261.4 29.4 %copy-start.22 = (f32[2,256,512]{2,1,0:T(8,128)S(1)}, f32[2,256,512]{2,1,0:T(8,128)}, u32[]{:S(2)}) copy-start(f32[2,256,512]{2,1,0:T(8,128)} %param.4) | copy-start | bytes 3145732
  261.4 29.3 %all-to-all-start.3 = ((f32[8,2,32,512]{3,2,1,0:T(8,128)}), f32[8,2,32,512]{3,2,1,0:T(8,128)S(1)}, u32[]{:S(2)}, u32[]{:S(2)}) async-start(f32[8,2,32,512]{3,2,1,0:T(8,128)} %bitcast_dynamic-update-slice_fusion), calls=%async_computation.3 | async-start | bytes 2097152 | tf_op jit(solution)/shard_map/all_to_all | solution.py:149
  (13 other events, 36.0 us)
